TPU v7x, 1024 devices: a whole 8x8x8 slice. The times are simulated.
1024 devices in a mesh: dp: 256 (over y, x_lo, z, core), tensor: 4 (over x_hi).
Axes of the slice: x: 8 (x_hi: 4, x_lo: 2; x = x_hi * 2 + x_lo), y: 8, z: 8, core: 2. Of those that a mesh axis runs over, the one named last changes fastest.
Arguments:
- train_hidden: bfloat16 [256, 128, 28672], P('dp', None, 'tensor'), may hold values from -6 to 6
- train_grad: bfloat16 [256, 128, 8192], P('dp', None, 'tensor'), may hold values from -6 to 6
- test_hidden: bfloat16 [256, 64, 28672], P('dp', None, 'tensor'), may hold values from -6 to 6
- test_grad: bfloat16 [256, 64, 8192], P('dp', None, 'tensor'), may hold values from -6 to 6
- proj_in: bfloat16 [64, 28672], P(None, 'tensor'), may hold values from -0.03125 to 0.03125
- proj_out: bfloat16 [64, 8192], P(None, 'tensor'), may hold values from -0.0625 to 0.0625
- precond_in: float32 [64, 64], replicated, may hold values from -0.75 to 0.75
- precond_out: float32 [64, 64], replicated, may hold values from -0.75 to 0.75
Outputs:
- scores: float32 [256, 256], P('dp', 'tensor')
All inputs are finite; a program needn't handle non-finite values.
Results may differ from a plain program's by a relative error of at most 0.0029.
Values may be sent and summed in bfloat16 or wider, within the bound.
No kernel may reach another device: no remote copies, remote signals or barrier semaphores. Data moves between devices by JAX's collectives and lax.ppermute only.
A program may use at most 32 MiB of HBM per device.

v0:
```python
import math

import jax
import jax.numpy as jnp
from jax import lax
from jax.sharding import PartitionSpec as P


def project(rows, factor):
    return lax.dot_general(
        rows, factor, (((1,), (1,)), ((), ())), preferred_element_type=jnp.float32
    )


def outer_sum(left, right, count, length, width):
    return jnp.einsum(
        "esi,esj->eij",
        left.reshape(count, length, width),
        right.reshape(count, length, width),
        precision=lax.Precision.HIGHEST,
    )


def condition(sketch, precond_in, precond_out):
    halfway = jnp.einsum("ai,qij->qaj", precond_in, sketch, precision=lax.Precision.HIGHEST)
    return jnp.einsum("qaj,jb->qab", halfway, precond_out, precision=lax.Precision.HIGHEST)


def shards(
    train_hidden, train_grad, test_hidden, test_grad, proj_in, proj_out, precond_in, precond_out
):
    ex_count, seq_len, hid_width = train_hidden.shape
    qry_count, qry_len, _ = test_hidden.shape
    feat_width = train_grad.shape[2]
    rank_width = proj_in.shape[0]
    left_train = project(train_hidden.reshape(ex_count * seq_len, hid_width), proj_in)
    right_train = project(train_grad.reshape(ex_count * seq_len, feat_width), proj_out)
    left_test = project(test_hidden.reshape(qry_count * qry_len, hid_width), proj_in)
    right_test = project(test_grad.reshape(qry_count * qry_len, feat_width), proj_out)
    right_train, right_test = lax.psum((right_train, right_test), "tensor")
    train_sketch = outer_sum(left_train, right_train, ex_count, seq_len, rank_width)
    test_sketch = outer_sum(left_test, right_test, qry_count, qry_len, rank_width)
    conditioned = condition(test_sketch, precond_in, precond_out)
    train_share, test_share = (
        lax.psum_scatter(train_sketch, "tensor", scatter_dimension=1, tiled=True),
        lax.psum_scatter(conditioned, "tensor", scatter_dimension=1, tiled=True),
    )
    test_share = test_share.astype(jnp.bfloat16)
    factor = 1.0 / (rank_width * math.sqrt(seq_len * qry_len))
    gathered = lax.all_gather(test_share, "dp", axis=0, tiled=True)
    partial_scores = (
        jnp.einsum(
            "eab,qab->eq",
            train_share,
            gathered.astype(jnp.float32),
            precision=lax.Precision.HIGHEST,
        )
        * factor
    )
    total = lax.psum(partial_scores, "tensor")
    kept = total.shape[1] // lax.axis_size("tensor")
    return lax.dynamic_slice_in_dim(total, lax.axis_index("tensor") * kept, kept, 1)


def solution(mesh):
    placed = (
        P("dp", None, "tensor"),
        P("dp", None, "tensor"),
        P("dp", None, "tensor"),
        P("dp", None, "tensor"),
        P(None, "tensor"),
        P(None, "tensor"),
        P(),
        P(),
    )
    return jax.shard_map(
        shards, mesh=mesh, in_specs=placed, out_specs=P("dp", "tensor"), check_vma=False
    )
```

profile of v0, /device:TPU:1, one launch (start us, length us, event | category | flops | bytes accessed | tf_op | source)
XLA Modules:
  0.0 402.9 jit_solution(13064679950630092824)
XLA Ops:
  6.5 0.0 copy-start
  6.5 0.0 reduce-scatter.5.cloned.1.call-start
  6.6 1.5 fusion.6
  8.1 1.2 fusion.8
  9.4 18.2 %all-reduce = (f32[128,64]{1,0:T(8,128)S(1)}, f32[64,64]{1,0:T(8,128)S(1)}) all-reduce(f32[128,64]{1,0:T(8,128)S(1)} %fusion.6, f32[64,64]{1,0:T(8,128)S(1)} %fusion.8), channel_id=1, replica_groups=mesh['dp'=256,'tensor'=4] {'tensor'}, use_global_device_ids=true, to_apply=%region_0.0 | all-reduce | flops 12288 | bytes 98304 | tf_op jit(solution)/shard_map/psum | solution.py:40
  27.6 1.8 fusion.4
  29.5 0.2 fusion.10
  29.7 0.0 copy-done.2
  29.7 0.2 convolution_bitcast_fusion.1
  30.0 0.0 copy-done.3
  30.0 0.8 convolution_bitcast_fusion
  30.8 0.0 reduce-scatter.5.cloned.1.call-update
  30.8 0.0 reduce-scatter.3.cloned.1.call-start
  30.9 0.0 copy-done
  30.9 0.0 copy-done.1
  30.9 0.6 fusion
  31.5 0.9 convolution_bitcast_fusion.2
  32.4 0.0 reduce-scatter.3.cloned.1.call-update
  32.4 38.8 %reduce-scatter.5.cloned.1.call-done = f32[1,16,64]{2,1,0:T(8,128)} async-done(((f32[1,64,64]{2,1,0:T(8,128)}), f32[1,16,64]{2,1,0:T(8,128)}) %reduce-scatter.5.cloned.1.call-update) | async-done | bytes 4112 | tf_op jit(solution)/shard_map/reduce_scatter | solution.py:46
  71.3 0.7 convert_element_type.4
  72.0 313.0 %all_gather.3 = bf16[256,16,64]{2,1,0:T(8,128)(2,1)S(1)} all-gather(bf16[1,16,64]{2,1,0:T(8,128)(2,1)S(1)} %convert_element_type.4), channel_id=1, replica_groups=mesh['dp'=256,'tensor'=4] {'dp'}, dimensions={0}, use_global_device_ids=true | all-gather | bytes 526336 | tf_op jit(solution)/shard_map/all_gather | solution.py:50
  384.9 1.6 fusion.2
  386.6 9.0 %psum.23 = f32[1,256]{1,0:T(1,128)S(1)} all-reduce(f32[1,256]{1,0:T(1,128)S(1)} %bitcast.43), channel_id=1, replica_groups=mesh['dp'=256,'tensor'=4] {'tensor'}, use_global_device_ids=true, to_apply=%region_4.0 | all-reduce | flops 256 | bytes 2048 | tf_op jit(solution)/shard_map/psum | solution.py:60
  395.5 0.6 constant_dynamic-slice_fusion
  (5 shorter events, 0.0 us)
Async XLA Ops:
  6.5 24.3 %copy-start = (bf16[1,128,7168]{2,1,0:T(8,128)(2,1)S(1)}, bf16[1,128,7168]{2,1,0:T(8,128)(2,1)}, u32[]{:S(2)}) copy-start(bf16[1,128,7168]{2,1,0:T(8,128)(2,1)} %param.8) | copy-start | bytes 5505028
  6.5 24.4 %copy-start.1 = (bf16[64,7168]{1,0:T(8,128)(2,1)S(1)}, bf16[64,7168]{1,0:T(8,128)(2,1)}, u32[]{:S(2)}) copy-start(bf16[64,7168]{1,0:T(8,128)(2,1)} %param.12) | copy-start | bytes 2752516
  6.5 23.2 %copy-start.2 = (f32[64,64]{1,0:T(8,128)S(1)}, f32[64,64]{1,0:T(8,128)}, u32[]{:S(2)}) copy-start(f32[64,64]{1,0:T(8,128)} %param.14) | copy-start | bytes 49156
  6.5 23.4 %copy-start.3 = (f32[64,64]{1,0:T(8,128)S(1)}, f32[64,64]{1,0:T(8,128)}, u32[]{:S(2)}) copy-start(f32[64,64]{1,0:T(8,128)} %param.15) | copy-start | bytes 49156
  6.5 64.7 %reduce-scatter.5.cloned.1.call-start = ((), (), s32[]{:S(2)}) async-start(), calls=%async_computation.3 | async-start | bytes 40960 | tf_op jit(solution)/shard_map/reduce_scatter | solution.py:46
  30.8 354.1 %reduce-scatter.3.cloned.1.call-start = ((), (), s32[]{:S(2)}) async-start(), calls=%async_computation.2 | async-start | bytes 40960 | tf_op jit(solution)/shard_map/reduce_scatter | solution.py:45
Sparse Core Ops, SparseCore 0:
  30.9 40.2 reduce-scatter.4
  74.6 29.1 reduce-scatter.2
where the time goes:
time: 403 us
  blocking collectives  340 us (84%)
  waiting for transfers between devices  38.9 us (10%)
  between operations  13.5 us (3%)
  matrix products  9.04 us (2%)
    all_gather x1, blocking collectives, shards(): gathered = lax.all_gather(test_share, 'dp', axis=0, tiled=True)  313 us
    reduce_scatter x1, waiting for transfers between devices, shards(): lax.psum_scatter(conditioned, 'tensor', scatter_dimension=1, tiled=True)  38.8 us
    psum x1, blocking collectives, shards(): right_train, right_test = lax.psum((right_train, right_test), 'tensor')  18.2 us
    psum x1, blocking collectives, shards(): total = lax.psum(partial_scores, 'tensor')  8.95 us
  transfers between devices with their start and end apart: 2, of which 1 were waited for; matrix products, arithmetic and copies ran while one was open for 1% of the time, Pallas kernels for 0%

commit v1 on v0

v1 whole, which is shorter than its diff:
```python
import functools
import math

import jax
import jax.numpy as jnp
from jax import lax
from jax.experimental import pallas as pl
from jax.experimental.pallas import tpu as pltpu
from jax.sharding import Mesh, PartitionSpec as P

Y, XL, Z, C, T = 8, 2, 8, 2, 4
OWN = XL * C
LINE = OWN * T
PLANE = Y * Z
F32, BF16 = jnp.float32, jnp.bfloat16
CHUNKS = 4


def nt(a, b, precision=None):
    return lax.dot_general(
        a, b, (((1,), (1,)), ((), ())), precision=precision, preferred_element_type=F32
    )


exact_nt = functools.partial(nt, precision=lax.Precision.HIGHEST)


def lanes_of(shape):
    return lax.broadcasted_iota(jnp.int32, shape, len(shape) - 1)


def rows_of(shape):
    return lax.broadcasted_iota(jnp.int32, shape, 0)


def hi_lo(x):
    hi = x.astype(BF16)
    lo = (x - hi.astype(F32)).astype(BF16)
    return jnp.concatenate([hi, lo], axis=1)


def project_kernel(
    th, tg, qh, qg, pin, pout, cin, cout, send, th_v, tg_v, qh_v, qg_v, pin_v, pout_v, cin_v, cout_v, sems
):
    count = 0
    groups = []

    def fetch(pairs):
        nonlocal count
        started = []
        for src, dst in pairs:
            copy = pltpu.make_async_copy(src, dst, sems.at[count])
            copy.start()
            started.append(copy)
            count += 1
        groups.append(started)

    fetch([(pout, pout_v), (tg.at[0], tg_v), (qg.at[0], qg_v)])
    step = th_v.shape[1] // CHUNKS
    for k in range(CHUNKS):
        cut = pl.ds(k * step, step)
        fetch(
            [
                (pin.at[:, cut], pin_v.at[:, cut]),
                (th.at[0, :, cut], th_v.at[:, cut]),
                (qh.at[0, :, cut], qh_v.at[:, cut]),
            ]
        )
        if k == 0:
            fetch([(cin, cin_v), (cout, cout_v)])

    def wait(group):
        for copy in group:
            copy.wait()

    wait(groups[0])
    right_train = nt(pout_v[...], tg_v[...])
    right_test = nt(pout_v[...], qg_v[...])
    wait(groups[1])
    wait(groups[2])
    right_test = lax.dot_general(
        cout_v[...], right_test, (((0,), (0,)), ((), ())),
        precision=lax.Precision.HIGHEST, preferred_element_type=F32,
    )
    left_train = left_test = None
    for k in range(CHUNKS):
        if k:
            wait(groups[k + 2])
        cut = pl.ds(k * step, step)
        more_train = nt(pin_v[:, cut], th_v[:, cut])
        more_test = nt(pin_v[:, cut], qh_v[:, cut])
        left_train = more_train if k == 0 else left_train + more_train
        left_test = more_test if k == 0 else left_test + more_test
    left_test = jnp.dot(
        cin_v[...], left_test, precision=lax.Precision.HIGHEST, preferred_element_type=F32
    )
    left_train, right_train = left_train.astype(BF16), right_train.astype(BF16)
    left_test, right_test = hi_lo(left_test), hi_lo(right_test)
    for i in range(OWN):
        for j in range(T):
            peer = i * T + j
            send[peer, 0:16] = left_train[16 * i : 16 * i + 16]
            send[peer, 16:32] = right_train[16 * j : 16 * j + 16]
            send[peer, 32:48] = left_test[16 * i : 16 * i + 16]
            send[peer, 48:64] = right_test[16 * j : 16 * j + 16]


def project(th, tg, qh, qg, pin, pout, cin, cout):
    any_space = pl.BlockSpec(memory_space=pl.ANY)
    vmem = lambda a: pltpu.VMEM(a.shape[-2:], a.dtype)
    args = (th, tg, qh, qg, pin, pout, cin, cout)
    return pl.pallas_call(
        project_kernel,
        out_shape=jax.ShapeDtypeStruct((LINE, 64, 128), BF16),
        in_specs=[any_space] * 8,
        out_specs=pl.BlockSpec(memory_space=pltpu.VMEM),
        scratch_shapes=[vmem(a) for a in args] + [pltpu.SemaphoreType.DMA((3 * CHUNKS + 5,))],
        name="project",
    )(*args)


def sketch_kernel(factor, recv, msg, train):
    lane = lanes_of((8, 128))
    lefts, rights = [], []
    for e in range(OWN):
        part = recv[T * e].astype(F32)
        for t in range(1, T):
            part = part + recv[T * e + t].astype(F32)
        left, right = part[0:16], part[16:32]
        block = exact_nt(left, jnp.concatenate([right] * 8, axis=0))
        train[e] = jnp.where(lane < 64, block[0:8], block[8:16]) * factor
        lefts.append(part[32:48])
        rights.append(part[48:64])
    left = jnp.concatenate(lefts, axis=0)
    right = jnp.concatenate(rights, axis=0)
    left = left + pltpu.roll(left, 64, 1)
    right = right + pltpu.roll(right, 64, 1)
    left = jnp.where(lanes_of((64, 128)) < 64, left, 0.0)
    block = exact_nt(left, jnp.concatenate([right, right], axis=0))
    same = rows_of((64, 128)) // 16 == (lanes_of((64, 128)) % 64) // 16
    block = jnp.where(same, block, 0.0)
    block = (block[0:16] + block[16:32]) + (block[32:48] + block[48:64])
    block = jnp.where(lane < 64, block[0:8], block[8:16]).astype(BF16)
    msg[...] = jnp.broadcast_to(block[None], msg.shape)


def sketch(recv, factor):
    vmem = pl.BlockSpec(memory_space=pltpu.VMEM)
    return pl.pallas_call(
        functools.partial(sketch_kernel, factor),
        out_shape=(
            jax.ShapeDtypeStruct((PLANE, 8, 128), BF16),
            jax.ShapeDtypeStruct((OWN, 8, 128), F32),
        ),
        in_specs=[vmem],
        out_specs=(vmem, vmem),
        name="sketch",
    )(recv)


def score_kernel(gathered, train, out, wide):
    wide[...] = gathered[...].astype(F32).reshape(PLANE * 8, 128)
    totals = [None] * OWN
    for r in range(8):
        rows = wide[pl.ds(r, PLANE, stride=8), :]
        for e in range(OWN):
            more = rows * train[e, r : r + 1, :]
            totals[e] = more if r == 0 else totals[e] + more
    total = jnp.concatenate(totals, axis=0)
    row, lane = rows_of((128, 64)), lanes_of((128, 64))
    pick = (row // 16) % OWN == (lane // 16) % XL * C + lane % C
    spread = jnp.dot(
        total, pick.astype(F32), precision=lax.Precision.HIGHEST, preferred_element_type=F32
    )
    row, lane = rows_of((OWN * PLANE, 64)), lanes_of((OWN * PLANE, 64))
    spread = jnp.where(row % 16 == lane // 32 * Z + (lane // C) % Z, spread, 0.0)
    out[...] = jnp.sum(spread.reshape(LINE, 16, 64), axis=1, keepdims=True)


def score(gathered, train):
    vmem = pl.BlockSpec(memory_space=pltpu.VMEM)
    return pl.pallas_call(
        score_kernel,
        out_shape=jax.ShapeDtypeStruct((LINE, 1, 64), F32),
        in_specs=[vmem, vmem],
        out_specs=vmem,
        scratch_shapes=[pltpu.VMEM((PLANE * 8, 128), F32)],
        name="score",
    )(gathered, train)


def exchange(x, axes):
    return lax.all_to_all(x, axes, split_axis=0, concat_axis=0, tiled=True)


def shards(
    train_hidden, train_grad, test_hidden, test_grad, proj_in, proj_out, precond_in, precond_out
):
    rank = proj_in.shape[0]
    factor = 1.0 / (rank * math.sqrt(train_hidden.shape[1] * test_hidden.shape[1]))
    send = project(
        train_hidden, train_grad, test_hidden, test_grad, proj_in, proj_out, precond_in, precond_out
    )
    recv = exchange(send, ("xl", "c", "t"))
    msg, train = sketch(recv, factor)
    gathered = exchange(msg, ("y", "z"))
    partial = score(gathered, train)
    total = exchange(partial, ("xl", "c", "t"))
    return jnp.sum(total, axis=0)


def solution(mesh):
    fine = Mesh(mesh.devices.reshape(Y, XL, Z, C, T), ("y", "xl", "z", "c", "t"))
    dp = ("y", "xl", "z", "c")
    placed = (
        P(dp, None, "t"),
        P(dp, None, "t"),
        P(dp, None, "t"),
        P(dp, None, "t"),
        P(None, "t"),
        P(None, "t"),
        P(),
        P(),
    )
    return jax.shard_map(
        shards, mesh=fine, in_specs=placed, out_specs=P(dp, "t"), check_vma=False
    )
```

time: 403 us -> 75.3 us (0.19)
  blocking collectives: 340 us -> 66.3 us
  waiting for transfers between devices: 38.9 us -> 0 us
  between operations: 13.5 us -> 0.01 us
  matrix products: 9.04 us -> 0 us
  Pallas kernels: 0 us -> 8.11 us
    all_gather x1 -> x0, blocking collectives: 313 us -> none  [shards(): gathered = lax.all_gather(test_share, 'dp', axis=0, tiled=True)]
    all_to_all x0 -> x3, blocking collectives: none -> 66.3 us  [exchange(): return lax.all_to_all(x, axes, split_axis=0, concat_axis=0, tiled=True)]
    reduce_scatter x2 -> x0, waiting for transfers between devices: 38.8 us -> none  [the longest x1 38.8 us: shards(): lax.psum_scatter(conditioned, 'tensor', scatter_dimension=1, tiled=True)]
    psum x2 -> x0, blocking collectives: 27.2 us -> none  [the longest x1 18.2 us: shards(): right_train, right_test = lax.psum((right_train, right_test), 'tensor')]
    dot_general x9 -> x0, matrix products: 9.04 us -> none  [the longest x4 5.25 us: project(): lax.dot_general(rows, factor, (((1,), (1,)), ((), ())), preferred_element...]
    pallas_call x0 -> x3, Pallas kernels: none -> 8.11 us  [the longest x1 4 us: project(): pl.pallas_call(project_kernel, out_shape=jax.ShapeDtypeStruct((LINE, 64,...]
  transfers between devices with their start and end apart: 2 -> 0, of which waited for: 1 -> 0; matrix products, arithmetic and copies ran while one was open for 1% -> 0% of each run, Pallas kernels for 0% -> 0%
where the time goes in v1:
time: 75.3 us; the launch traced here: 75 us
  blocking collectives  66.3 us (88%)
  Pallas kernels  8.11 us (11%)
    all_to_all x3, blocking collectives, exchange(): return lax.all_to_all(x, axes, split_axis=0, concat_axis=0, tiled=True)  66.3 us
    pallas_call x1, Pallas kernels, project(): pl.pallas_call(project_kernel, out_shape=jax.ShapeDtypeStruct((LINE, 64,...  4 us
    pallas_call x1, Pallas kernels, sketch(): pl.pallas_call(functools.partial(sketch_kernel, factor), out_shape=(jax.S...  2.26 us
    pallas_call x1, Pallas kernels, score(): pl.pallas_call(score_kernel, out_shape=jax.ShapeDtypeStruct((LINE, 1, 64)...  1.86 us

profile of v1, /device:TPU:1, one launch (start us, length us, event | category | flops | bytes accessed | tf_op | source)
XLA Modules:
  0.0 75.0 jit_solution(1818452853017008493)
XLA Ops:
  0.0 4.0 %project.1 = bf16[16,64,128]{2,1,0:T(8,128)(2,1)} custom-call(bf16[1,128,7168]{2,1,0:T(8,128)(2,1)} %th.1, bf16[1,128,2048]{2,1,0:T(8,128)(2,1)} %tg.1, bf16[1,64,7168]{2,1,0:T(8,128)(2,1)} %qh.1, bf16[1,64,2048]{2,1,0:T(8,128)(2,1)} %qg.1, bf16[64,7168]{1,0:T(8,128)(2,1)} %pin.1, bf16[64,2048]{1,0:T(8,128)(2,1)} %pout.1, f32[64,64]{1,0:T(8,128)} %cin.1, ...), custom_call_target="tpu_custom_call" | custom-call | tf_op jit(solution)/shard_map/project/pallas_call | solution.py:112
  4.0 30.2 %all_to_all.15.recv = bf16[16,64,128]{2,1,0:T(8,128)(2,1)} all-to-all(bf16[16,64,128]{2,1,0:T(8,128)(2,1)} %project.1), channel_id=1, replica_groups=mesh['y'=8,'xl'=2,'z'=8,'c'=2,'t'=4] {'xl','c','t'}, dimensions={0} | all-to-all | bytes 524288 | tf_op jit(solution)/shard_map/all_to_all | solution.py:193
  34.2 2.3 %sketch.1 = (bf16[64,8,128]{2,1,0:T(8,128)(2,1)}, f32[4,8,128]{2,1,0:T(8,128)}) custom-call(bf16[16,64,128]{2,1,0:T(8,128)(2,1)} %all_to_all.15.recv), custom_call_target="tpu_custom_call" | custom-call | tf_op jit(solution)/shard_map/sketch/pallas_call | solution.py:149
  36.5 25.3 %all_to_all.16.gathered = bf16[64,8,128]{2,1,0:T(8,128)(2,1)} all-to-all(bf16[64,8,128]{2,1,0:T(8,128)(2,1)} %get-tuple-element.7), channel_id=1, replica_groups=mesh['y'=8,'xl'=2,'z'=8,'c'=2,'t'=4] {'y','z'}, dimensions={0} | all-to-all | bytes 262144 | tf_op jit(solution)/shard_map/all_to_all | solution.py:193
  61.7 1.9 %score.1 = f32[16,1,64]{2,1,0:T(1,128)} custom-call(bf16[64,8,128]{2,1,0:T(8,128)(2,1)} %all_to_all.16.gathered, f32[4,8,128]{2,1,0:T(8,128)} %get-tuple-element.8.train), custom_call_target="tpu_custom_call" | custom-call | tf_op jit(solution)/shard_map/score/pallas_call | solution.py:182
  63.6 10.9 %all_to_all.17 = f32[16,1,64]{2,1,0:T(1,128)S(1)} all-to-all(f32[16,1,64]{2,1,0:T(1,128)} %score.1), channel_id=1, replica_groups=mesh['y'=8,'xl'=2,'z'=8,'c'=2,'t'=4] {'xl','c','t'}, dimensions={0} | all-to-all | bytes 8192 | tf_op jit(solution)/shard_map/all_to_all | solution.py:193
  74.4 0.5 reduce_sum.11

commit v2 on v1

--- a/solution.py
+++ b/solution.py
@@ -106,15 +106,18 @@
 
 
 def project(th, tg, qh, qg, pin, pout, cin, cout):
-    any_space = pl.BlockSpec(memory_space=pl.ANY)
+    hbm = pl.BlockSpec(memory_space=pltpu.HBM)
     vmem = lambda a: pltpu.VMEM(a.shape[-2:], a.dtype)
-    args = (th, tg, qh, qg, pin, pout, cin, cout)
+    args = [
+        pltpu.with_memory_space_constraint(a, pltpu.HBM) for a in (th, tg, qh, qg, pin, pout, cin, cout)
+    ]
     return pl.pallas_call(
         project_kernel,
         out_shape=jax.ShapeDtypeStruct((LINE, 64, 128), BF16),
-        in_specs=[any_space] * 8,
+        in_specs=[hbm] * 8,
         out_specs=pl.BlockSpec(memory_space=pltpu.VMEM),
         scratch_shapes=[vmem(a) for a in args] + [pltpu.SemaphoreType.DMA((3 * CHUNKS + 5,))],
+        compiler_params=pltpu.CompilerParams(vmem_limit_bytes=12 << 20),
         name="project",
     )(*args)
 
@@ -154,6 +157,7 @@
         ),
         in_specs=[vmem],
         out_specs=(vmem, vmem),
+        compiler_params=pltpu.CompilerParams(vmem_limit_bytes=4 << 20),
         name="sketch",
     )(recv)
 
@@ -185,6 +189,7 @@
         in_specs=[vmem, vmem],
         out_specs=vmem,
         scratch_shapes=[pltpu.VMEM((PLANE * 8, 128), F32)],
+        compiler_params=pltpu.CompilerParams(vmem_limit_bytes=4 << 20),
         name="score",
     )(gathered, train)
 

time: 75.3 us -> 70.5 us (0.936)
  Pallas kernels: 8.11 us -> 4.29 us
  blocking collectives: 66.3 us -> 65.5 us
    pallas_call x1, Pallas kernels: 2.26 us -> 0.64 us  [sketch(): pl.pallas_call(functools.partial(sketch_kernel, factor), out_shape=(jax.S...]
    pallas_call x1, Pallas kernels: 1.86 us -> 0.35 us  [score(): pl.pallas_call(score_kernel, out_shape=jax.ShapeDtypeStruct((LINE, 1, 64)...]
    all_to_all x3, blocking collectives: 66.3 us -> 65.5 us  [exchange(): return lax.all_to_all(x, axes, split_axis=0, concat_axis=0, tiled=True)]
where the time goes in v2:
time: 70.5 us; the launch traced here: 70.3 us
  blocking collectives  65.5 us (93%)
  Pallas kernels  4.29 us (6%)
    all_to_all x3, blocking collectives, exchange(): return lax.all_to_all(x, axes, split_axis=0, concat_axis=0, tiled=True)  65.5 us
    pallas_call x1, Pallas kernels, project(): pl.pallas_call(project_kernel, out_shape=jax.ShapeDtypeStruct((LINE, 64,...  3.3 us

profile of v2, /device:TPU:1, one launch (start us, length us, event | category | flops | bytes accessed | tf_op | source)
XLA Modules:
  0.0 70.3 jit_solution(10186334673141725413)
XLA Ops:
  0.0 3.3 %project.1 = bf16[16,64,128]{2,1,0:T(8,128)(2,1)S(1)} custom-call(bf16[1,128,7168]{2,1,0:T(8,128)(2,1)} %th.1, bf16[1,128,2048]{2,1,0:T(8,128)(2,1)} %tg.1, bf16[1,64,7168]{2,1,0:T(8,128)(2,1)} %qh.1, bf16[1,64,2048]{2,1,0:T(8,128)(2,1)} %qg.1, bf16[64,7168]{1,0:T(8,128)(2,1)} %pin.1, bf16[64,2048]{1,0:T(8,128)(2,1)} %pout.1, f32[64,64]{1,0:T(8,128)} %cin.1, ...), custom_call_target="tpu_custom_call" | custom-call | tf_op jit(solution)/shard_map/project/pallas_call | solution.py:114
  3.3 28.6 %all_to_all.15.recv = bf16[16,64,128]{2,1,0:T(8,128)(2,1)S(1)} all-to-all(bf16[16,64,128]{2,1,0:T(8,128)(2,1)S(1)} %project.1), channel_id=1, replica_groups=mesh['y'=8,'xl'=2,'z'=8,'c'=2,'t'=4] {'xl','c','t'}, dimensions={0} | all-to-all | bytes 524288 | tf_op jit(solution)/shard_map/all_to_all | solution.py:198
  31.9 0.6 sketch.1
  32.5 26.2 %all_to_all.16.gathered = bf16[64,8,128]{2,1,0:T(8,128)(2,1)S(1)} all-to-all(bf16[64,8,128]{2,1,0:T(8,128)(2,1)S(1)} %get-tuple-element.7), channel_id=1, replica_groups=mesh['y'=8,'xl'=2,'z'=8,'c'=2,'t'=4] {'y','z'}, dimensions={0} | all-to-all | bytes 262144 | tf_op jit(solution)/shard_map/all_to_all | solution.py:198
  58.8 0.3 score.1
  59.2 10.6 %all_to_all.17 = f32[16,1,64]{2,1,0:T(1,128)S(1)} all-to-all(f32[16,1,64]{2,1,0:T(1,128)S(1)} %score.1), channel_id=1, replica_groups=mesh['y'=8,'xl'=2,'z'=8,'c'=2,'t'=4] {'xl','c','t'}, dimensions={0} | all-to-all | bytes 8192 | tf_op jit(solution)/shard_map/all_to_all | solution.py:198
  69.8 0.5 reduce_sum.11

commit v3 on v2

--- a/solution.py
+++ b/solution.py
@@ -12,6 +12,8 @@
 OWN = XL * C
 LINE = OWN * T
 PLANE = Y * Z
+LATE_Y, LATE_Z, LATE_T = 4, 7, 2
+AXES = ("y", "xl", "z", "c", "t")
 F32, BF16 = jnp.float32, jnp.bfloat16
 CHUNKS = 4
 
@@ -177,7 +179,8 @@
         total, pick.astype(F32), precision=lax.Precision.HIGHEST, preferred_element_type=F32
     )
     row, lane = rows_of((OWN * PLANE, 64)), lanes_of((OWN * PLANE, 64))
-    spread = jnp.where(row % 16 == lane // 32 * Z + (lane // C) % Z, spread, 0.0)
+    at_z = (lane // C % Z + Z - LATE_Z) % Z
+    spread = jnp.where(row % 16 == lane // 32 * Z + at_z, spread, 0.0)
     out[...] = jnp.sum(spread.reshape(LINE, 16, 64), axis=1, keepdims=True)
 
 
@@ -194,8 +197,27 @@
     )(gathered, train)
 
 
-def exchange(x, axes):
-    return lax.all_to_all(x, axes, split_axis=0, concat_axis=0, tiled=True)
+def place(y, xl, z, c, t):
+    return (((y * XL + xl) * Z + z) * C + c) * T + t
+
+
+LINES = [
+    [place(y, xl, z, c, (t + LATE_T) % T) for xl in range(XL) for c in range(C) for t in range(T)]
+    for y in range(Y)
+    for z in range(Z)
+]
+PLANES = [
+    [place((y + LATE_Y) % Y, xl, (z + LATE_Z) % Z, c, t) for y in range(Y) for z in range(Z)]
+    for xl in range(XL)
+    for c in range(C)
+    for t in range(T)
+]
+
+
+def exchange(x, groups):
+    return lax.all_to_all(
+        x, AXES, split_axis=0, concat_axis=0, axis_index_groups=groups, tiled=True
+    )
 
 
 def shards(
@@ -206,11 +228,11 @@
     send = project(
         train_hidden, train_grad, test_hidden, test_grad, proj_in, proj_out, precond_in, precond_out
     )
-    recv = exchange(send, ("xl", "c", "t"))
+    recv = exchange(send, LINES)
     msg, train = sketch(recv, factor)
-    gathered = exchange(msg, ("y", "z"))
+    gathered = exchange(msg, PLANES)
     partial = score(gathered, train)
-    total = exchange(partial, ("xl", "c", "t"))
+    total = exchange(partial, LINES)
     return jnp.sum(total, axis=0)
 
 

time: 70.5 us -> 61.5 us (0.87)
  blocking collectives: 65.5 us -> 56.5 us
    all_to_all x3, blocking collectives: 65.5 us -> 56.5 us  [exchange(): lax.all_to_all(x, AXES, split_axis=0, concat_axis=0, axis_index_groups=gr...]
where the time goes in v3:
time: 61.5 us; the launch traced here: 61.3 us
  blocking collectives  56.5 us (92%)
  Pallas kernels  4.29 us (7%)
    all_to_all x3, blocking collectives, exchange(): lax.all_to_all(x, AXES, split_axis=0, concat_axis=0, axis_index_groups=gr...  56.5 us
    pallas_call x1, Pallas kernels, project(): pl.pallas_call(project_kernel, out_shape=jax.ShapeDtypeStruct((LINE, 64,...  3.3 us

profile of v3, /device:TPU:1, one launch (start us, length us, event | category | flops | bytes accessed | tf_op | source)
XLA Modules:
  0.0 61.3 jit_solution(8351126317704118825)
XLA Ops:
  0.0 3.3 %project.1 = bf16[16,64,128]{2,1,0:T(8,128)(2,1)S(1)} custom-call(bf16[1,128,7168]{2,1,0:T(8,128)(2,1)} %th.1, bf16[1,128,2048]{2,1,0:T(8,128)(2,1)} %tg.1, bf16[1,64,7168]{2,1,0:T(8,128)(2,1)} %qh.1, bf16[1,64,2048]{2,1,0:T(8,128)(2,1)} %qg.1, bf16[64,7168]{1,0:T(8,128)(2,1)} %pin.1, bf16[64,2048]{1,0:T(8,128)(2,1)} %pout.1, f32[64,64]{1,0:T(8,128)} %cin.1, ...), custom_call_target="tpu_custom_call" | custom-call | tf_op jit(solution)/shard_map/project/pallas_call | solution.py:116
  3.3 27.5 %all_to_all.15.recv = bf16[16,64,128]{2,1,0:T(8,128)(2,1)S(1)} all-to-all(bf16[16,64,128]{2,1,0:T(8,128)(2,1)S(1)} %project.1), channel_id=1, replica_groups={{2,3,0,1,6,7,4,5,66,67,64,65,70,71,68,69},{10,11,8,9,14,15,12,13,74,75,..., dimensions={0} | all-to-all | bytes 524288 | tf_op jit(solution)/shard_map/all_to_all | solution.py:218
  30.8 0.6 %sketch.1 = (bf16[64,8,128]{2,1,0:T(8,128)(2,1)S(1)}, f32[4,8,128]{2,1,0:T(8,128)S(1)}) custom-call(bf16[16,64,128]{2,1,0:T(8,128)(2,1)S(1)} %all_to_all.15.recv), custom_call_target="tpu_custom_call" | custom-call | tf_op jit(solution)/shard_map/sketch/pallas_call | solution.py:154
  31.5 19.1 %all_to_all.16.gathered = bf16[64,8,128]{2,1,0:T(8,128)(2,1)S(1)} all-to-all(bf16[64,8,128]{2,1,0:T(8,128)(2,1)S(1)} %get-tuple-element.7), channel_id=1, replica_groups={{568,512,520,528,536,544,552,560,696,640,648,656,664,672,680,688,824,76..., dimensions={0} | all-to-all | bytes 262144 | tf_op jit(solution)/shard_map/all_to_all | solution.py:218
  50.5 0.3 score.1
  50.9 9.9 %all_to_all.17 = f32[16,1,64]{2,1,0:T(1,128)S(1)} all-to-all(f32[16,1,64]{2,1,0:T(1,128)S(1)} %score.1), channel_id=1, replica_groups={{2,3,0,1,6,7,4,5,66,67,64,65,70,71,68,69},{10,11,8,9,14,15,12,13,74,75,..., dimensions={0} | all-to-all | bytes 8192 | tf_op jit(solution)/shard_map/all_to_all | solution.py:218
  60.8 0.5 reduce_sum.11

commit v4 on v3

--- a/solution.py
+++ b/solution.py
@@ -12,7 +12,7 @@
 OWN = XL * C
 LINE = OWN * T
 PLANE = Y * Z
-LATE_Y, LATE_Z, LATE_T = 4, 7, 2
+LATE_Y, LATE_Z, LATE_T = 4, 5, 2
 AXES = ("y", "xl", "z", "c", "t")
 F32, BF16 = jnp.float32, jnp.bfloat16
 CHUNKS = 4

time: 61.5 us -> 60.8 us (0.989)
  blocking collectives: 56.5 us -> 55.7 us
    all_to_all x3, blocking collectives: 56.5 us -> 55.7 us  [exchange(): lax.all_to_all(x, AXES, split_axis=0, concat_axis=0, axis_index_groups=gr...]
where the time goes in v4:
time: 60.8 us; the launch traced here: 60.6 us
  blocking collectives  55.7 us (92%)
  Pallas kernels  4.29 us (7%)
    all_to_all x3, blocking collectives, exchange(): lax.all_to_all(x, AXES, split_axis=0, concat_axis=0, axis_index_groups=gr...  55.7 us
    pallas_call x1, Pallas kernels, project(): pl.pallas_call(project_kernel, out_shape=jax.ShapeDtypeStruct((LINE, 64,...  3.3 us

profile of v4, /device:TPU:1, one launch (start us, length us, event | category | flops | bytes accessed | tf_op | source)
XLA Modules:
  0.0 60.6 jit_solution(13341435705034748446)
XLA Ops:
  0.0 3.3 %project.1 = bf16[16,64,128]{2,1,0:T(8,128)(2,1)S(1)} custom-call(bf16[1,128,7168]{2,1,0:T(8,128)(2,1)} %th.1, bf16[1,128,2048]{2,1,0:T(8,128)(2,1)} %tg.1, bf16[1,64,7168]{2,1,0:T(8,128)(2,1)} %qh.1, bf16[1,64,2048]{2,1,0:T(8,128)(2,1)} %qg.1, bf16[64,7168]{1,0:T(8,128)(2,1)} %pin.1, bf16[64,2048]{1,0:T(8,128)(2,1)} %pout.1, f32[64,64]{1,0:T(8,128)} %cin.1, ...), custom_call_target="tpu_custom_call" | custom-call | tf_op jit(solution)/shard_map/project/pallas_call | solution.py:116
  3.3 27.5 %all_to_all.15.recv = bf16[16,64,128]{2,1,0:T(8,128)(2,1)S(1)} all-to-all(bf16[16,64,128]{2,1,0:T(8,128)(2,1)S(1)} %project.1), channel_id=1, replica_groups={{2,3,0,1,6,7,4,5,66,67,64,65,70,71,68,69},{10,11,8,9,14,15,12,13,74,75,..., dimensions={0} | all-to-all | bytes 524288 | tf_op jit(solution)/shard_map/all_to_all | solution.py:218
  30.8 0.6 %sketch.1 = (bf16[64,8,128]{2,1,0:T(8,128)(2,1)S(1)}, f32[4,8,128]{2,1,0:T(8,128)S(1)}) custom-call(bf16[16,64,128]{2,1,0:T(8,128)(2,1)S(1)} %all_to_all.15.recv), custom_call_target="tpu_custom_call" | custom-call | tf_op jit(solution)/shard_map/sketch/pallas_call | solution.py:154
  31.5 18.2 %all_to_all.16.gathered = bf16[64,8,128]{2,1,0:T(8,128)(2,1)S(1)} all-to-all(bf16[64,8,128]{2,1,0:T(8,128)(2,1)S(1)} %get-tuple-element.7), channel_id=1, replica_groups={{552,560,568,512,520,528,536,544,680,688,696,640,648,656,664,672,808,81..., dimensions={0} | all-to-all | bytes 262144 | tf_op jit(solution)/shard_map/all_to_all | solution.py:218
  49.6 0.3 score.1
  50.0 10.1 %all_to_all.17 = f32[16,1,64]{2,1,0:T(1,128)S(1)} all-to-all(f32[16,1,64]{2,1,0:T(1,128)S(1)} %score.1), channel_id=1, replica_groups={{2,3,0,1,6,7,4,5,66,67,64,65,70,71,68,69},{10,11,8,9,14,15,12,13,74,75,..., dimensions={0} | all-to-all | bytes 8192 | tf_op jit(solution)/shard_map/all_to_all | solution.py:218
  60.0 0.5 reduce_sum.11

commit v5 on v4

--- a/solution.py
+++ b/solution.py
@@ -15,13 +15,23 @@
 LATE_Y, LATE_Z, LATE_T = 4, 5, 2
 AXES = ("y", "xl", "z", "c", "t")
 F32, BF16 = jnp.float32, jnp.bfloat16
-CHUNKS = 4
+PARTS = (10, 8, 6, 4)
+SPLIT = 2
 
 
 def nt(a, b, precision=None):
     return lax.dot_general(
         a, b, (((1,), (1,)), ((), ())), precision=precision, preferred_element_type=F32
     )
+
+
+def wide_nt(a, b):
+    step = a.shape[1] // SPLIT
+    total = None
+    for k in range(SPLIT):
+        more = nt(a[:, k * step : (k + 1) * step], b[:, k * step : (k + 1) * step])
+        total = more if k == 0 else total + more
+    return total
 
 
 exact_nt = functools.partial(nt, precision=lax.Precision.HIGHEST)
@@ -58,9 +68,11 @@
         groups.append(started)
 
     fetch([(pout, pout_v), (tg.at[0], tg_v), (qg.at[0], qg_v)])
-    step = th_v.shape[1] // CHUNKS
-    for k in range(CHUNKS):
-        cut = pl.ds(k * step, step)
+    cuts, low = [], 0
+    for part in PARTS:
+        cuts.append(pl.ds(low, th_v.shape[1] * part // sum(PARTS)))
+        low += cuts[-1].size
+    for k, cut in enumerate(cuts):
         fetch(
             [
                 (pin.at[:, cut], pin_v.at[:, cut]),
@@ -76,8 +88,8 @@
             copy.wait()
 
     wait(groups[0])
-    right_train = nt(pout_v[...], tg_v[...])
-    right_test = nt(pout_v[...], qg_v[...])
+    right_train = wide_nt(pout_v[...], tg_v[...])
+    right_test = wide_nt(pout_v[...], qg_v[...])
     wait(groups[1])
     wait(groups[2])
     right_test = lax.dot_general(
@@ -85,12 +97,11 @@
         precision=lax.Precision.HIGHEST, preferred_element_type=F32,
     )
     left_train = left_test = None
-    for k in range(CHUNKS):
+    for k, cut in enumerate(cuts):
         if k:
             wait(groups[k + 2])
-        cut = pl.ds(k * step, step)
-        more_train = nt(pin_v[:, cut], th_v[:, cut])
-        more_test = nt(pin_v[:, cut], qh_v[:, cut])
+        more_train = wide_nt(pin_v[:, cut], th_v[:, cut])
+        more_test = wide_nt(pin_v[:, cut], qh_v[:, cut])
         left_train = more_train if k == 0 else left_train + more_train
         left_test = more_test if k == 0 else left_test + more_test
     left_test = jnp.dot(
@@ -118,7 +129,7 @@
         out_shape=jax.ShapeDtypeStruct((LINE, 64, 128), BF16),
         in_specs=[hbm] * 8,
         out_specs=pl.BlockSpec(memory_space=pltpu.VMEM),
-        scratch_shapes=[vmem(a) for a in args] + [pltpu.SemaphoreType.DMA((3 * CHUNKS + 5,))],
+        scratch_shapes=[vmem(a) for a in args] + [pltpu.SemaphoreType.DMA((3 * len(PARTS) + 5,))],
         compiler_params=pltpu.CompilerParams(vmem_limit_bytes=12 << 20),
         name="project",
     )(*args)
@@ -197,6 +208,22 @@
     )(gathered, train)
 
 
+def total_kernel(parts, out):
+    out[...] = jnp.sum(parts[...], axis=0)
+
+
+def total(parts):
+    vmem = pl.BlockSpec(memory_space=pltpu.VMEM)
+    return pl.pallas_call(
+        total_kernel,
+        out_shape=jax.ShapeDtypeStruct(parts.shape[1:], F32),
+        in_specs=[vmem],
+        out_specs=vmem,
+        compiler_params=pltpu.CompilerParams(vmem_limit_bytes=1 << 20),
+        name="total",
+    )(parts)
+
+
 def place(y, xl, z, c, t):
     return (((y * XL + xl) * Z + z) * C + c) * T + t
 
@@ -232,8 +259,7 @@
     msg, train = sketch(recv, factor)
     gathered = exchange(msg, PLANES)
     partial = score(gathered, train)
-    total = exchange(partial, LINES)
-    return jnp.sum(total, axis=0)
+    return total(exchange(partial, LINES))
 
 
 def solution(mesh):

time: 60.8 us -> 60.7 us (level)
  no operation moved by 1% of the time
where the time goes in v5:
time: 60.7 us; the launch traced here: 60.4 us
  blocking collectives  55.7 us (92%)
  Pallas kernels  4.69 us (8%)
    all_to_all x3, blocking collectives, exchange(): lax.all_to_all(x, AXES, split_axis=0, concat_axis=0, axis_index_groups=gr...  55.7 us
    pallas_call x1, Pallas kernels, project(): pl.pallas_call(project_kernel, out_shape=jax.ShapeDtypeStruct((LINE, 64,...  3.17 us

profile of v5, /device:TPU:1, one launch (start us, length us, event | category | flops | bytes accessed | tf_op | source)
XLA Modules:
  0.0 60.4 jit_solution(7401427793250383590)
XLA Ops:
  0.0 3.2 %project.1 = bf16[16,64,128]{2,1,0:T(8,128)(2,1)S(1)} custom-call(bf16[1,128,7168]{2,1,0:T(8,128)(2,1)} %th.1, bf16[1,128,2048]{2,1,0:T(8,128)(2,1)} %tg.1, bf16[1,64,7168]{2,1,0:T(8,128)(2,1)} %qh.1, bf16[1,64,2048]{2,1,0:T(8,128)(2,1)} %qg.1, bf16[64,7168]{1,0:T(8,128)(2,1)} %pin.1, bf16[64,2048]{1,0:T(8,128)(2,1)} %pout.1, f32[64,64]{1,0:T(8,128)} %cin.1, ...), custom_call_target="tpu_custom_call" | custom-call | tf_op jit(solution)/shard_map/project/pallas_call | solution.py:127
  3.2 27.5 %all_to_all.15.recv = bf16[16,64,128]{2,1,0:T(8,128)(2,1)S(1)} all-to-all(bf16[16,64,128]{2,1,0:T(8,128)(2,1)S(1)} %project.1), channel_id=1, replica_groups={{2,3,0,1,6,7,4,5,66,67,64,65,70,71,68,69},{10,11,8,9,14,15,12,13,74,75,..., dimensions={0} | all-to-all | bytes 524288 | tf_op jit(solution)/shard_map/all_to_all | solution.py:245
  30.7 0.6 %sketch.1 = (bf16[64,8,128]{2,1,0:T(8,128)(2,1)S(1)}, f32[4,8,128]{2,1,0:T(8,128)S(1)}) custom-call(bf16[16,64,128]{2,1,0:T(8,128)(2,1)S(1)} %all_to_all.15.recv), custom_call_target="tpu_custom_call" | custom-call | tf_op jit(solution)/shard_map/sketch/pallas_call | solution.py:165
  31.3 18.2 %all_to_all.16.gathered = bf16[64,8,128]{2,1,0:T(8,128)(2,1)S(1)} all-to-all(bf16[64,8,128]{2,1,0:T(8,128)(2,1)S(1)} %get-tuple-element.7), channel_id=1, replica_groups={{552,560,568,512,520,528,536,544,680,688,696,640,648,656,664,672,808,81..., dimensions={0} | all-to-all | bytes 262144 | tf_op jit(solution)/shard_map/all_to_all | solution.py:245
  49.5 0.3 score.1
  49.9 10.1 %all_to_all.17.parts = f32[16,1,64]{2,1,0:T(1,128)S(1)} all-to-all(f32[16,1,64]{2,1,0:T(1,128)S(1)} %score.1), channel_id=1, replica_groups={{2,3,0,1,6,7,4,5,66,67,64,65,70,71,68,69},{10,11,8,9,14,15,12,13,74,75,..., dimensions={0} | all-to-all | bytes 8192 | tf_op jit(solution)/shard_map/all_to_all | solution.py:245
  59.9 0.5 total.1

commit v6 on v5

--- a/solution.py
+++ b/solution.py
@@ -34,7 +34,7 @@
     return total
 
 
-exact_nt = functools.partial(nt, precision=lax.Precision.HIGHEST)
+exact_nt = functools.partial(nt, precision=lax.Precision.HIGH)
 
 
 def lanes_of(shape):
@@ -94,7 +94,7 @@
     wait(groups[2])
     right_test = lax.dot_general(
         cout_v[...], right_test, (((0,), (0,)), ((), ())),
-        precision=lax.Precision.HIGHEST, preferred_element_type=F32,
+        precision=lax.Precision.HIGH, preferred_element_type=F32,
     )
     left_train = left_test = None
     for k, cut in enumerate(cuts):
@@ -105,7 +105,7 @@
         left_train = more_train if k == 0 else left_train + more_train
         left_test = more_test if k == 0 else left_test + more_test
     left_test = jnp.dot(
-        cin_v[...], left_test, precision=lax.Precision.HIGHEST, preferred_element_type=F32
+        cin_v[...], left_test, precision=lax.Precision.HIGH, preferred_element_type=F32
     )
     left_train, right_train = left_train.astype(BF16), right_train.astype(BF16)
     left_test, right_test = hi_lo(left_test), hi_lo(right_test)
@@ -187,7 +187,7 @@
     row, lane = rows_of((128, 64)), lanes_of((128, 64))
     pick = (row // 16) % OWN == (lane // 16) % XL * C + lane % C
     spread = jnp.dot(
-        total, pick.astype(F32), precision=lax.Precision.HIGHEST, preferred_element_type=F32
+        total, pick.astype(F32), precision=lax.Precision.HIGH, preferred_element_type=F32
     )
     row, lane = rows_of((OWN * PLANE, 64)), lanes_of((OWN * PLANE, 64))
     at_z = (lane // C % Z + Z - LATE_Z) % Z

time: 60.7 us -> 60.2 us (level)
  no operation moved by 1% of the time
where the time goes in v6:
time: 60.2 us; the launch traced here: 60 us
  blocking collectives  55.7 us (93%)
  Pallas kernels  4.31 us (7%)
    all_to_all x3, blocking collectives, exchange(): lax.all_to_all(x, AXES, split_axis=0, concat_axis=0, axis_index_groups=gr...  55.7 us
    pallas_call x1, Pallas kernels, project(): pl.pallas_call(project_kernel, out_shape=jax.ShapeDtypeStruct((LINE, 64,...  3.11 us

profile of v6, /device:TPU:1, one launch (start us, length us, event | category | flops | bytes accessed | tf_op | source)
XLA Modules:
  0.0 60.0 jit_solution(2645986672054187772)
XLA Ops:
  0.0 3.1 %project.1 = bf16[16,64,128]{2,1,0:T(8,128)(2,1)S(1)} custom-call(bf16[1,128,7168]{2,1,0:T(8,128)(2,1)} %th.1, bf16[1,128,2048]{2,1,0:T(8,128)(2,1)} %tg.1, bf16[1,64,7168]{2,1,0:T(8,128)(2,1)} %qh.1, bf16[1,64,2048]{2,1,0:T(8,128)(2,1)} %qg.1, bf16[64,7168]{1,0:T(8,128)(2,1)} %pin.1, bf16[64,2048]{1,0:T(8,128)(2,1)} %pout.1, f32[64,64]{1,0:T(8,128)} %cin.1, ...), custom_call_target="tpu_custom_call" | custom-call | tf_op jit(solution)/shard_map/project/pallas_call | solution.py:127
  3.1 27.5 %all_to_all.15.recv = bf16[16,64,128]{2,1,0:T(8,128)(2,1)S(1)} all-to-all(bf16[16,64,128]{2,1,0:T(8,128)(2,1)S(1)} %project.1), channel_id=1, replica_groups={{2,3,0,1,6,7,4,5,66,67,64,65,70,71,68,69},{10,11,8,9,14,15,12,13,74,75,..., dimensions={0} | all-to-all | bytes 524288 | tf_op jit(solution)/shard_map/all_to_all | solution.py:245
  30.6 0.4 sketch.1
  31.0 18.2 %all_to_all.16.gathered = bf16[64,8,128]{2,1,0:T(8,128)(2,1)S(1)} all-to-all(bf16[64,8,128]{2,1,0:T(8,128)(2,1)S(1)} %get-tuple-element.7), channel_id=1, replica_groups={{552,560,568,512,520,528,536,544,680,688,696,640,648,656,664,672,808,81..., dimensions={0} | all-to-all | bytes 262144 | tf_op jit(solution)/shard_map/all_to_all | solution.py:245
  49.2 0.3 score.1
  49.5 10.1 %all_to_all.17.parts = f32[16,1,64]{2,1,0:T(1,128)S(1)} all-to-all(f32[16,1,64]{2,1,0:T(1,128)S(1)} %score.1), channel_id=1, replica_groups={{2,3,0,1,6,7,4,5,66,67,64,65,70,71,68,69},{10,11,8,9,14,15,12,13,74,75,..., dimensions={0} | all-to-all | bytes 8192 | tf_op jit(solution)/shard_map/all_to_all | solution.py:245
  59.5 0.5 total.1

commit v7 on v6

--- a/solution.py
+++ b/solution.py
@@ -183,7 +183,7 @@
         for e in range(OWN):
             more = rows * train[e, r : r + 1, :]
             totals[e] = more if r == 0 else totals[e] + more
-    total = jnp.concatenate(totals, axis=0)
+    total = jnp.concatenate([totals[e ^ 1] for e in range(OWN)], axis=0)
     row, lane = rows_of((128, 64)), lanes_of((128, 64))
     pick = (row // 16) % OWN == (lane // 16) % XL * C + lane % C
     spread = jnp.dot(
@@ -230,6 +230,11 @@
 
 LINES = [
     [place(y, xl, z, c, (t + LATE_T) % T) for xl in range(XL) for c in range(C) for t in range(T)]
+    for y in range(Y)
+    for z in range(Z)
+]
+LAST_LINES = [
+    [place(y, xl, z, C - 1 - c, (t + LATE_T) % T) for xl in range(XL) for c in range(C) for t in range(T)]
     for y in range(Y)
     for z in range(Z)
 ]
@@ -259,7 +264,7 @@
     msg, train = sketch(recv, factor)
     gathered = exchange(msg, PLANES)
     partial = score(gathered, train)
-    return total(exchange(partial, LINES))
+    return total(exchange(partial, LAST_LINES))
 
 
 def solution(mesh):

time: 60.2 us -> 60 us (level)
  no operation moved by 1% of the time
where the time goes in v7:
time: 60 us; the launch traced here: 59.8 us
  blocking collectives  55.4 us (92%)
  Pallas kernels  4.31 us (7%)
    all_to_all x3, blocking collectives, exchange(): lax.all_to_all(x, AXES, split_axis=0, concat_axis=0, axis_index_groups=gr...  55.4 us
    pallas_call x1, Pallas kernels, project(): pl.pallas_call(project_kernel, out_shape=jax.ShapeDtypeStruct((LINE, 64,...  3.11 us

profile of v7, /device:TPU:1, one launch (start us, length us, event | category | flops | bytes accessed | tf_op | source)
XLA Modules:
  0.0 59.8 jit_solution(3403583610433072210)
XLA Ops:
  0.0 3.1 %project.1 = bf16[16,64,128]{2,1,0:T(8,128)(2,1)S(1)} custom-call(bf16[1,128,7168]{2,1,0:T(8,128)(2,1)} %th.1, bf16[1,128,2048]{2,1,0:T(8,128)(2,1)} %tg.1, bf16[1,64,7168]{2,1,0:T(8,128)(2,1)} %qh.1, bf16[1,64,2048]{2,1,0:T(8,128)(2,1)} %qg.1, bf16[64,7168]{1,0:T(8,128)(2,1)} %pin.1, bf16[64,2048]{1,0:T(8,128)(2,1)} %pout.1, f32[64,64]{1,0:T(8,128)} %cin.1, ...), custom_call_target="tpu_custom_call" | custom-call | tf_op jit(solution)/shard_map/project/pallas_call | solution.py:127
  3.1 27.5 %all_to_all.15.recv = bf16[16,64,128]{2,1,0:T(8,128)(2,1)S(1)} all-to-all(bf16[16,64,128]{2,1,0:T(8,128)(2,1)S(1)} %project.1), channel_id=1, replica_groups={{2,3,0,1,6,7,4,5,66,67,64,65,70,71,68,69},{10,11,8,9,14,15,12,13,74,75,..., dimensions={0} | all-to-all | bytes 524288 | tf_op jit(solution)/shard_map/all_to_all | solution.py:250
  30.6 0.4 sketch.1
  31.0 18.2 %all_to_all.16.gathered = bf16[64,8,128]{2,1,0:T(8,128)(2,1)S(1)} all-to-all(bf16[64,8,128]{2,1,0:T(8,128)(2,1)S(1)} %get-tuple-element.7), channel_id=1, replica_groups={{552,560,568,512,520,528,536,544,680,688,696,640,648,656,664,672,808,81..., dimensions={0} | all-to-all | bytes 262144 | tf_op jit(solution)/shard_map/all_to_all | solution.py:250
  49.2 0.3 score.1
  49.5 9.8 %all_to_all.17.parts = f32[16,1,64]{2,1,0:T(1,128)S(1)} all-to-all(f32[16,1,64]{2,1,0:T(1,128)S(1)} %score.1), channel_id=1, replica_groups={{6,7,4,5,2,3,0,1,70,71,68,69,66,67,64,65},{14,15,12,13,10,11,8,9,78,79,..., dimensions={0} | all-to-all | bytes 8192 | tf_op jit(solution)/shard_map/all_to_all | solution.py:250
  59.2 0.5 total.1
